TPU v7x, 256 devices: a whole 4x4x8 slice. The times are simulated.
256 devices in a mesh: xg: 4 (over x_hi, core), yd: 64 (over x_lo, z, y).
Axes of the slice: x: 4 (x_hi: 2, x_lo: 2; x = x_hi * 2 + x_lo), y: 4, z: 8, core: 2. Of those that a mesh axis runs over, the one named last changes fastest.
Arguments:
- mobile: float32 [4096, 1, 1024], P('yd', None, 'xg'), may hold values from 0 to 2
- dispersion_x: float32 [4096, 1, 1024], P('yd', None, 'xg'), may hold values from 0.5 to 200000
- dispersion_y: float32 [4096, 1, 1024], P('yd', None, 'xg'), may hold values from 0.5 to 200000
- capacity: float32 [4096, 1, 1024], P('yd', None, 'xg'), may hold values from 0.5 to 8
- immobile: float32 [4, 4096, 1, 1024], P(None, 'yd', None, 'xg'), may hold values from 0 to 2
- exchange_rates: float32 [4], replicated, may hold values from 0.02 to 50
- rate_shares: float32 [4], replicated, may hold values from 0.1 to 1
Outputs:
- updated: float32 [4096, 1, 1024], P('yd', None, 'xg')
All inputs are finite; a program needn't handle non-finite values.
Results may differ from a plain program's by a relative error of at most 0.0003.
Values sent between devices are 32-bit elements; how exact they have to be, the bound alone decides.
A program may use at most 64 MiB of HBM per device.

v0:
```python
import jax
import jax.numpy as jnp
from jax import lax
from jax.sharding import PartitionSpec as P


def shifted_2(value, axis, steps):
    count = lax.axis_size(axis)
    pairs = [(source, (source + steps) % count) for source in range(count)]
    return lax.ppermute(value, axis, pairs)


def shifted(values, stride, axis, filling):
    length = values.shape[axis]
    if stride > 0:
        kept_part = lax.slice_in_dim(values, 0, length - stride, axis=axis)
        filler = jnp.full_like(lax.slice_in_dim(values, 0, stride, axis=axis), filling)
        return jnp.concatenate([filler, kept_part], axis=axis)
    backward = -stride
    kept_part = lax.slice_in_dim(values, backward, length, axis=axis)
    filler = jnp.full_like(lax.slice_in_dim(values, 0, backward, axis=axis), filling)
    return jnp.concatenate([kept_part, filler], axis=axis)


def pick_at(values, position, axis):
    return lax.index_in_dim(values, position, axis, keepdims=False)


def periodic_solve(face_coef, storage, right_side, axis):
    length = right_side.shape[axis]
    sub_coef = -face_coef
    super_coef = -jnp.roll(face_coef, -1, axis)
    main_coef = storage + face_coef - super_coef
    stride = 1
    while stride < length // 2:
        sub_left = jnp.roll(sub_coef, stride, axis)
        main_left = jnp.roll(main_coef, stride, axis)
        super_left = jnp.roll(super_coef, stride, axis)
        side_left = jnp.roll(right_side, stride, axis)
        sub_right = jnp.roll(sub_coef, -stride, axis)
        main_right = jnp.roll(main_coef, -stride, axis)
        super_right = jnp.roll(super_coef, -stride, axis)
        side_right = jnp.roll(right_side, -stride, axis)
        left_ratio = sub_coef / main_left
        right_ratio = super_coef / main_right
        main_coef = main_coef - left_ratio * super_left - right_ratio * sub_right
        right_side = right_side - left_ratio * side_left - right_ratio * side_right
        sub_coef = -left_ratio * sub_left
        super_coef = -right_ratio * super_right
        stride = stride * 2
    coupling = sub_coef + super_coef
    main_other = jnp.roll(main_coef, stride, axis)
    coupling_other = jnp.roll(coupling, stride, axis)
    side_other = jnp.roll(right_side, stride, axis)
    return (right_side * main_other - coupling * side_other) / (
        main_coef * main_other - coupling * coupling_other
    )


def block_solve(face_coef, storage, source, axis):
    length = source.shape[axis]
    position = lax.broadcasted_iota(jnp.int32, source.shape, axis)
    at_first = position == 0
    at_last = position == length - 1
    following = shifted(face_coef, -1, axis, 0.0)
    nothing = jnp.zeros_like(source)
    sub_coef = jnp.where(at_first | at_last, nothing, -face_coef)
    super_coef = jnp.where(at_last, nothing, -following)
    main_coef = jnp.where(at_last, 1.0, storage + face_coef + following)
    right_side = jnp.stack(
        [
            jnp.where(at_last, nothing, source),
            jnp.where(at_first, face_coef, nothing),
            jnp.where(at_last, 1.0, nothing),
        ]
    )
    stride = 1
    while stride < length:
        sub_left = shifted(sub_coef, stride, axis, 0.0)
        main_left = shifted(main_coef, stride, axis, 1.0)
        super_left = shifted(super_coef, stride, axis, 0.0)
        side_left = shifted(right_side, stride, axis + 1, 0.0)
        sub_right = shifted(sub_coef, -stride, axis, 0.0)
        main_right = shifted(main_coef, -stride, axis, 1.0)
        super_right = shifted(super_coef, -stride, axis, 0.0)
        side_right = shifted(right_side, -stride, axis + 1, 0.0)
        left_ratio = sub_coef / main_left
        right_ratio = super_coef / main_right
        right_side = right_side - left_ratio[None] * side_left - right_ratio[None] * side_right
        main_coef = main_coef - left_ratio * super_left - right_ratio * sub_right
        sub_coef = -left_ratio * sub_left
        super_coef = -right_ratio * super_right
        stride = stride * 2
    return right_side / main_coef[None]


def reduced_rows(solved, face_coef, storage, source, upcoming, axis):
    from_next, face_next = upcoming
    length = source.shape[axis]
    face_last = pick_at(face_coef, length - 1, axis)
    sub_last = -face_last
    super_last = -face_next
    main_last = pick_at(storage, length - 1, axis) + face_last + face_next
    coef_prev = sub_last * pick_at(solved[1], length - 2, axis)
    coef_self = (
        main_last + sub_last * pick_at(solved[2], length - 2, axis) + super_last * from_next[1]
    )
    coef_next = super_last * from_next[2]
    target = (
        pick_at(source, length - 1, axis)
        - sub_last * pick_at(solved[0], length - 2, axis)
        - super_last * from_next[0]
    )
    return (coef_prev, coef_self, coef_next, target)


def dense_cyclic(all_rows, group_size):
    matrix_rows = []
    targets = []
    for row_index in range(group_size):
        entries = [jnp.zeros_like(all_rows[row_index, 1]) for column in range(group_size)]
        entries[(row_index - 1) % group_size] = all_rows[row_index, 0]
        entries[row_index] = all_rows[row_index, 1]
        entries[(row_index + 1) % group_size] = all_rows[row_index, 2]
        matrix_rows.append(entries)
        targets.append(all_rows[row_index, 3])
    for pivot in range(group_size):
        for row_index in range(pivot + 1, group_size):
            factor = matrix_rows[row_index][pivot] / matrix_rows[pivot][pivot]
            matrix_rows[row_index] = [
                matrix_rows[row_index][column] - factor * matrix_rows[pivot][column]
                for column in range(group_size)
            ]
            targets[row_index] = targets[row_index] - factor * targets[pivot]
    solutions = [None] * group_size
    for row_index in reversed(range(group_size)):
        total = targets[row_index]
        for column in range(row_index + 1, group_size):
            total = total - matrix_rows[row_index][column] * solutions[column]
        solutions[row_index] = total / matrix_rows[row_index][row_index]
    return jnp.stack(solutions)


def local(mobile, dispersion_x, dispersion_y, capacity, immobile, exchange_rates, rate_shares):
    weights = rate_shares * exchange_rates / (1.0 + exchange_rates)
    gain_terms = capacity[None] * weights[:, None, None, None]
    storage = 1.0 + jnp.sum(gain_terms, axis=0)
    source = mobile + jnp.sum(gain_terms * immobile, axis=0)
    solved = block_solve(dispersion_x, storage, source, 2)
    head_values = pick_at(solved, 0, 3)
    upcoming = shifted_2((head_values, pick_at(dispersion_x, 0, 2)), "xg", -1)
    rows = reduced_rows(solved, dispersion_x, storage, source, upcoming, 2)
    group_size = lax.axis_size("xg")
    all_rows = lax.all_gather(jnp.stack(rows)[None], "xg", axis=0, tiled=True)
    solutions = dense_cyclic(all_rows, group_size)
    own_index = lax.axis_index("xg")
    own_value = lax.dynamic_index_in_dim(solutions, own_index, 0, keepdims=False)
    prev_value = lax.dynamic_index_in_dim(
        solutions, (own_index + group_size - 1) % group_size, 0, keepdims=False
    )
    after_x = solved[0] + solved[1] * prev_value[..., None] + solved[2] * own_value[..., None]
    group_count = lax.axis_size("yd")

    def regroup(values):
        return values.reshape(values.shape[0], group_count, -1)

    line_values = lax.all_to_all(regroup(after_x), "yd", split_axis=1, concat_axis=0, tiled=True)
    line_faces = lax.all_to_all(
        regroup(dispersion_y), "yd", split_axis=1, concat_axis=0, tiled=True
    )
    line_storage = lax.all_to_all(regroup(storage), "yd", split_axis=1, concat_axis=0, tiled=True)
    solved_lines = periodic_solve(line_faces, line_storage, line_storage * line_values, 0)
    updated = lax.all_to_all(solved_lines, "yd", split_axis=0, concat_axis=1, tiled=True)
    updated = updated.reshape(after_x.shape)
    return updated


def solution(mesh):
    return jax.shard_map(
        local,
        mesh=mesh,
        in_specs=(
            P("yd", None, "xg"),
            P("yd", None, "xg"),
            P("yd", None, "xg"),
            P("yd", None, "xg"),
            P(None, "yd", None, "xg"),
            P(),
            P(),
        ),
        out_specs=P("yd", None, "xg"),
        check_vma=False,
    )
```

profile of v0, /device:TPU:4, one launch (start us, length us, event | category | flops | bytes accessed | tf_op | source)
XLA Modules:
  0.0 107.0 jit_solution(12925277914980473333)
XLA Ops:
  0.0 0.8 copy.95
  0.9 0.8 copy.55
  1.8 0.7 add_divide_fusion
  2.5 1.6 %fusion = (f32[64,256]{1,0:T(8,128)S(1)}, f32[64,256]{1,0:T(8,128)S(1)}) fusion(f32[4,64,1,256]{3,2,1,0:T(1,128)} %param.11, f32[64,256]{1,0:T(8,128)S(1)} %bitcast.400, f32[4]{0:T(128)S(1)} %add_divide_fusion), kind=kLoop, calls=%fused_computation.2 | loop fusion | flops 229376 | bytes 458768 | tf_op jit(solution)/shard_map/reduce_sum | solution.py:148
  4.1 0.9 add_select_fusion
  5.1 0.9 fusion.90
  6.2 0.1 multiply_subtract_fusion.13
  6.4 0.1 fusion.91
  6.7 0.1 multiply_subtract_fusion.12
  6.9 0.1 fusion.93
  7.3 0.1 multiply_subtract_fusion.11
  7.5 0.1 fusion.95
  7.8 0.1 multiply_subtract_fusion.10
  8.0 0.1 fusion.97
  8.3 0.1 multiply_subtract_fusion.9
  8.5 0.1 fusion.99
  8.9 0.1 multiply_subtract_fusion.8
  9.1 0.1 fusion.101
  9.9 0.1 multiply_subtract_fusion.6
  10.1 0.1 multiply_subtract_fusion.5
  10.4 0.1 multiply_subtract_fusion.4
  10.6 0.1 multiply_subtract_fusion.3
  10.9 0.1 multiply_subtract_fusion.2
  11.1 0.1 multiply_subtract_fusion.1
  11.3 0.1 multiply_subtract_fusion
  11.8 0.6 slice_reduce_fusion.1
  12.3 2.4 %collective-permute-start = (f32[64,1]{0,1:T(1,128)S(1)}, f32[64,1]{0,1:T(1,128)S(1)}, u32[]{:S(2)}, u32[]{:S(2)}) collective-permute-start(f32[64,1]{0,1:T(1,128)S(1)} %bitcast.403), channel_id=1, source_target_pairs={{0,192},{64,0},{128,64},{192,128},{1,193},{65,1},{129,65},{193,129... | collective-permute-start | bytes 776 | tf_op jit(solution)/shard_map/ppermute | solution.py:10
  14.8 0.8 reshape.21111
  15.6 11.9 %all-to-all-start.2 = ((f32[64,1,256]{2,1,0:T(1,128)}), f32[64,1,256]{2,1,0:T(1,128)S(1)}, u32[]{:S(2)}, u32[]{:S(2)}) async-start(f32[64,1,256]{2,1,0:T(1,128)} %reshape.21111), calls=%async_computation.2 | async-start | bytes 131072 | tf_op jit(solution)/shard_map/all_to_all | solution.py:168
  27.6 0.2 fusion.53
  28.2 0.8 reshape.21113
  29.0 6.7 %all-gather = f32[16,64,1]{1,2,0:T(1,128)S(1)} all-gather(f32[4,64,1]{1,2,0:T(1,128)S(1)} %pad_maximum_fusion.2), channel_id=2, replica_groups=mesh['xg'=4,'yd'=64] {'xg'}, dimensions={0}, use_global_device_ids=true | all-gather | bytes 5120 | tf_op jit(solution)/shard_map/all_gather | solution.py:154
  35.9 0.8 reshape.21115
  36.6 1.7 %all-to-all-done.2 = f32[64,1,256]{2,1,0:T(1,128)S(1)} async-done(((f32[64,1,256]{2,1,0:T(1,128)}), f32[64,1,256]{2,1,0:T(1,128)S(1)}, u32[]{:S(2)}, u32[]{:S(2)}) %all-to-all-start.2) | async-done | bytes 65568 | tf_op jit(solution)/shard_map/all_to_all | solution.py:168
  38.3 9.6 %all-to-all-start = ((f32[64,1,256]{2,1,0:T(1,128)}), f32[64,1,256]{2,1,0:T(1,128)S(1)}, u32[]{:S(2)}, u32[]{:S(2)}) async-start(f32[64,1,256]{2,1,0:T(1,128)} %reshape.21113), calls=%async_computation | async-start | bytes 131072 | tf_op jit(solution)/shard_map/all_to_all | solution.py:171
  47.9 0.6 broadcast.430
  48.5 0.8 reduce.15
  49.3 0.1 reshape.21112
  49.6 9.1 %all-to-all-done = f32[64,1,256]{2,1,0:T(1,128)S(1)} async-done(((f32[64,1,256]{2,1,0:T(1,128)}), f32[64,1,256]{2,1,0:T(1,128)S(1)}, u32[]{:S(2)}, u32[]{:S(2)}) %all-to-all-start) | async-done | bytes 65568 | tf_op jit(solution)/shard_map/all_to_all | solution.py:171
  58.7 4.8 %all-to-all-start.1 = ((f32[64,1,256]{2,1,0:T(1,128)}), f32[64,1,256]{2,1,0:T(1,128)S(1)}, u32[]{:S(2)}, u32[]{:S(2)}) async-start(f32[64,1,256]{2,1,0:T(1,128)} %reshape.21115), calls=%async_computation.1 | async-start | bytes 131072 | tf_op jit(solution)/shard_map/all_to_all | solution.py:167
  63.5 0.8 reduce.14
  64.3 0.1 reshape.21114
  64.5 9.5 %all-to-all-done.1 = f32[64,1,256]{2,1,0:T(1,128)S(1)} async-done(((f32[64,1,256]{2,1,0:T(1,128)}), f32[64,1,256]{2,1,0:T(1,128)S(1)}, u32[]{:S(2)}, u32[]{:S(2)}) %all-to-all-start.1) | async-done | bytes 65568 | tf_op jit(solution)/shard_map/all_to_all | solution.py:167
  74.1 0.8 reduce.16
  74.9 0.1 reshape.21116
  75.6 0.1 fusion.2
  76.5 0.2 fusion.6
  77.5 0.2 fusion.10
  78.5 0.2 fusion.14
  79.5 0.2 fusion.18
  80.5 0.2 fusion.22
  81.5 0.2 fusion.26
  82.2 0.1 fusion.30
  82.6 0.1 fusion.34
  82.9 0.1 fusion.38
  83.3 0.1 fusion.42
  83.7 0.6 reduce.17
  84.3 0.6 copy.96
  85.0 1.7 %reshape.21117 = f32[64,1,256]{2,1,0:T(1,128)S(1)} reshape(f32[4096,4]{1,0:T(8,128)S(1)} %copy.96) | data formatting | bytes 131072
  86.7 14.6 %all_to_all.69 = f32[64,1,256]{2,1,0:T(1,128)S(1)} all-to-all(f32[64,1,256]{2,1,0:T(1,128)S(1)} %reshape.21117), channel_id=1, replica_groups=mesh['xg'=4,'yd'=64] {'yd'}, dimensions={0} | all-to-all | bytes 131072 | tf_op jit(solution)/shard_map/all_to_all | solution.py:173
  101.3 0.8 reduce.18
  102.1 3.4 %reshape.21118 = f32[4096,1,4]{2,1,0:T(1,128)S(1)} reshape(f32[64,256]{1,0:T(8,128)S(1)} %reduce.18) | data formatting | bytes 131072
  105.5 0.7 copy.86
  106.3 0.7 copy.85
  (188 shorter events, 10.7 us)
Async XLA Ops:
  0.0 6.0 %copy-start = (f32[64,1,256]{2,1,0:T(1,128)S(1)}, f32[64,1,256]{2,1,0:T(1,128)}, u32[]{:S(2)}) copy-start(f32[64,1,256]{2,1,0:T(1,128)} %param.8) | copy-start | bytes 196612
  11.1 3.6 %copy-start.1 = (f32[64,1,256]{2,1,0:T(1,128)S(1)}, f32[64,1,256]{2,1,0:T(1,128)}, u32[]{:S(2)}) copy-start(f32[64,1,256]{2,1,0:T(1,128)} %param.9) | copy-start | bytes 196612
  11.7 17.3 %collective-permute-start.1 = (f32[3,64,1]{1,2,0:T(1,128)S(1)}, f32[3,64,1]{1,2,0:T(1,128)S(1)}, u32[]{:S(2)}, u32[]{:S(2)}) collective-permute-start(f32[3,64,1]{1,2,0:T(1,128)S(1)} %squeeze.95), channel_id=1, source_target_pairs={{0,192},{64,0},{128,64},{192,128},{1,193},{65,1},{129,65},{193,129... | collective-permute-start | bytes 2312 | tf_op jit(solution)/shard_map/ppermute | solution.py:10
  12.3 16.7 %collective-permute-start = (f32[64,1]{0,1:T(1,128)S(1)}, f32[64,1]{0,1:T(1,128)S(1)}, u32[]{:S(2)}, u32[]{:S(2)}) collective-permute-start(f32[64,1]{0,1:T(1,128)S(1)} %bitcast.403), channel_id=1, source_target_pairs={{0,192},{64,0},{128,64},{192,128},{1,193},{65,1},{129,65},{193,129... | collective-permute-start | bytes 776 | tf_op jit(solution)/shard_map/ppermute | solution.py:10
  15.6 22.7 %all-to-all-start.2 = ((f32[64,1,256]{2,1,0:T(1,128)}), f32[64,1,256]{2,1,0:T(1,128)S(1)}, u32[]{:S(2)}, u32[]{:S(2)}) async-start(f32[64,1,256]{2,1,0:T(1,128)} %reshape.21111), calls=%async_computation.2 | async-start | bytes 131072 | tf_op jit(solution)/shard_map/all_to_all | solution.py:168
  38.3 20.4 %all-to-all-start = ((f32[64,1,256]{2,1,0:T(1,128)}), f32[64,1,256]{2,1,0:T(1,128)S(1)}, u32[]{:S(2)}, u32[]{:S(2)}) async-start(f32[64,1,256]{2,1,0:T(1,128)} %reshape.21113), calls=%async_computation | async-start | bytes 131072 | tf_op jit(solution)/shard_map/all_to_all | solution.py:171
  58.7 15.4 %all-to-all-start.1 = ((f32[64,1,256]{2,1,0:T(1,128)}), f32[64,1,256]{2,1,0:T(1,128)S(1)}, u32[]{:S(2)}, u32[]{:S(2)}) async-start(f32[64,1,256]{2,1,0:T(1,128)} %reshape.21115), calls=%async_computation.1 | async-start | bytes 131072 | tf_op jit(solution)/shard_map/all_to_all | solution.py:167
where the time goes:
time: 108 us; the launch traced here: 107 us
  starting transfers between devices  28.8 us (27%)
  local copies, waits for them, and re-layouts  21.3 us (20%)
  blocking collectives  21.3 us (20%)
  waiting for transfers between devices  20.3 us (19%)
  other arithmetic  14.1 us (13%)
  between operations  1.29 us (1%)
    all_to_all x1, blocking collectives, local(): lax.all_to_all(solved_lines, 'yd', split_axis=0, concat_axis=1, tiled=True)  14.6 us
    all_to_all x1, starting transfers between devices, local(): lax.all_to_all(regroup(dispersion_y), 'yd', split_axis=1, concat_axis=0,...  11.9 us
    unnamed x16, local copies, waits for them, and re-layouts  10.2 us
    all_to_all x1, starting transfers between devices, local(): lax.all_to_all(regroup(storage), 'yd', split_axis=1, concat_axis=0, tiled...  9.63 us
    all_to_all x1, waiting for transfers between devices, local(): lax.all_to_all(regroup(after_x), 'yd', split_axis=1, concat_axis=0, tiled...  9.53 us
    all_to_all x1, waiting for transfers between devices, local(): lax.all_to_all(regroup(storage), 'yd', split_axis=1, concat_axis=0, tiled...  9.06 us
    all_gather x1, blocking collectives, local(): all_rows = lax.all_gather(jnp.stack(rows)[None], 'xg', axis=0, tiled=True)  6.7 us
    all_to_all x1, starting transfers between devices, local(): lax.all_to_all(regroup(after_x), 'yd', split_axis=1, concat_axis=0, tiled...  4.8 us
  transfers between devices with their start and end apart: 5, of which 3 were waited for; matrix products, arithmetic and copies ran while one was open for 6% of the time, Pallas kernels for 0%

commit v1 on v0

--- a/solution.py
+++ b/solution.py
@@ -2,6 +2,7 @@
 import jax.numpy as jnp
 from jax import lax
 from jax.sharding import PartitionSpec as P
+from jax.lax import all_to_all, axis_size
 
 
 def shifted_2(value, axis, steps):
@@ -170,7 +171,15 @@
     )
     line_storage = lax.all_to_all(regroup(storage), "yd", split_axis=1, concat_axis=0, tiled=True)
     solved_lines = periodic_solve(line_faces, line_storage, line_storage * line_values, 0)
-    updated = lax.all_to_all(solved_lines, "yd", split_axis=0, concat_axis=1, tiled=True)
+    updated = jnp.concatenate(
+        all_to_all(
+            jnp.stack(jnp.split(solved_lines, axis_size("yd"), axis=0)),
+            axis_name="yd",
+            split_axis=0,
+            concat_axis=0,
+        ),
+        axis=1,
+    )
     updated = updated.reshape(after_x.shape)
     return updated
 

time: 108 us -> 102 us (0.944)
  other arithmetic: 14.1 us -> 10.3 us
  local copies, waits for them, and re-layouts: 21.3 us -> 19.1 us
  waiting for transfers between devices: 20.3 us -> 18.5 us
  blocking collectives: 21.3 us -> 22.5 us
  starting transfers between devices: 28.8 us -> 30 us
    all_to_all x1, starting transfers between devices: 9.63 us -> 11.3 us  [local(): lax.all_to_all(regroup(storage), 'yd', split_axis=1, concat_axis=0, tiled...]
    all_to_all x1, waiting for transfers between devices: 1.66 us -> 0.01 us  [local(): lax.all_to_all(regroup(dispersion_y), 'yd', split_axis=1, concat_axis=0,...]
    unnamed x16 -> x86, local copies, waits for them, and re-layouts: 10.2 us -> 8.61 us
    ppermute x2, starting transfers between devices: 2.44 us -> 1.04 us  [shifted_2(): return lax.ppermute(value, axis, pairs)]
    all_gather x1, blocking collectives: 6.7 us -> 7.96 us  [local(): all_rows = lax.all_gather(jnp.stack(rows)[None], 'xg', axis=0, tiled=True)]
  transfers between devices with their start and end apart: 5 -> 5, of which waited for: 3 -> 2; matrix products, arithmetic and copies ran while one was open for 6% -> 12% of each run, Pallas kernels for 0% -> 0%
where the time goes in v1:
time: 102 us
  starting transfers between devices  30 us (29%)
  blocking collectives  22.5 us (22%)
  local copies, waits for them, and re-layouts  19.1 us (19%)
  waiting for transfers between devices  18.5 us (18%)
  other arithmetic  10.3 us (10%)
  between operations  1.36 us (1%)
    all_to_all x1, blocking collectives, local(): all_to_all(jnp.stack(jnp.split(solved_lines, axis_size('yd'), axis=0)), a...  14.6 us
    all_to_all x1, starting transfers between devices, local(): lax.all_to_all(regroup(dispersion_y), 'yd', split_axis=1, concat_axis=0,...  12.9 us
    all_to_all x1, starting transfers between devices, local(): lax.all_to_all(regroup(storage), 'yd', split_axis=1, concat_axis=0, tiled...  11.3 us
    all_to_all x1, waiting for transfers between devices, local(): lax.all_to_all(regroup(after_x), 'yd', split_axis=1, concat_axis=0, tiled...  9.5 us
    all_to_all x1, waiting for transfers between devices, local(): lax.all_to_all(regroup(storage), 'yd', split_axis=1, concat_axis=0, tiled...  8.99 us
    unnamed x86, local copies, waits for them, and re-layouts  8.61 us
    all_gather x1, blocking collectives, local(): all_rows = lax.all_gather(jnp.stack(rows)[None], 'xg', axis=0, tiled=True)  7.96 us
    all_to_all x1, starting transfers between devices, local(): lax.all_to_all(regroup(after_x), 'yd', split_axis=1, concat_axis=0, tiled...  4.78 us
  transfers between devices with their start and end apart: 5, of which 2 were waited for; matrix products, arithmetic and copies ran while one was open for 12% of the time, Pallas kernels for 0%

profile of v1, /device:TPU:4, one launch (start us, length us, event | category | flops | bytes accessed | tf_op | source)
XLA Modules:
  0.0 101.7 jit_solution(14564751586257472106)
XLA Ops:
  0.0 0.9 copy.232
  0.9 0.8 reshape.21110
  1.7 12.9 %all-to-all-start.2 = ((f32[64,1,256]{2,1,0:T(1,128)}), f32[64,1,256]{2,1,0:T(1,128)S(1)}, u32[]{:S(2)}, u32[]{:S(2)}) async-start(f32[64,1,256]{2,1,0:T(1,128)} %reshape.21110), calls=%async_computation.2 | async-start | bytes 131072 | tf_op jit(solution)/shard_map/all_to_all | solution.py:169
  14.7 0.8 copy-done
  15.6 0.6 copy-done.4
  16.2 0.7 fusion
  17.1 0.7 copy-done.2
  18.0 0.1 multiply_subtract_fusion.6
  18.1 0.1 fusion.110
  18.4 0.1 multiply_subtract_fusion.13
  18.6 0.1 fusion.91
  18.8 0.1 multiply_subtract_fusion.5
  19.2 0.1 multiply_subtract_fusion.12
  19.4 0.1 fusion.93
  19.5 0.1 multiply_subtract_fusion.4
  19.9 0.1 multiply_subtract_fusion.11
  20.2 0.1 fusion.95
  20.3 0.1 multiply_subtract_fusion.3
  20.7 0.1 multiply_subtract_fusion.10
  21.0 0.1 fusion.97
  21.1 0.1 multiply_subtract_fusion.2
  21.5 0.1 multiply_subtract_fusion.9
  21.7 0.1 fusion.99
  21.9 0.1 multiply_subtract_fusion.1
  22.3 0.1 multiply_subtract_fusion.8
  22.5 0.1 fusion.101
  22.7 0.1 multiply_subtract_fusion
  23.0 0.1 multiply_subtract_fusion.7
  23.6 0.6 slice_reduce_fusion.1
  24.1 1.0 collective-permute-start
  25.1 0.2 fusion.53
  25.5 0.8 reshape.21112
  26.6 8.0 %all-gather = f32[16,64,1]{1,2,0:T(1,128)S(1)} all-gather(f32[4,64,1]{1,2,0:T(1,128)S(1)} %pad_maximum_fusion.2), channel_id=2, replica_groups=mesh['xg'=4,'yd'=64] {'xg'}, dimensions={0}, use_global_device_ids=true | all-gather | bytes 5120 | tf_op jit(solution)/shard_map/all_gather | solution.py:155
  34.7 0.8 reshape.21114
  35.5 11.3 %all-to-all-start = ((f32[64,1,256]{2,1,0:T(1,128)}), f32[64,1,256]{2,1,0:T(1,128)S(1)}, u32[]{:S(2)}, u32[]{:S(2)}) async-start(f32[64,1,256]{2,1,0:T(1,128)} %reshape.21112), calls=%async_computation | async-start | bytes 131072 | tf_op jit(solution)/shard_map/all_to_all | solution.py:172
  46.8 0.6 broadcast.430
  47.3 0.8 reduce.15
  48.2 0.1 reshape.21111
  48.3 0.1 all_to_all.53
  48.5 9.0 %all-to-all-done = f32[64,1,256]{2,1,0:T(1,128)S(1)} async-done(((f32[64,1,256]{2,1,0:T(1,128)}), f32[64,1,256]{2,1,0:T(1,128)S(1)}, u32[]{:S(2)}, u32[]{:S(2)}) %all-to-all-start) | async-done | bytes 65568 | tf_op jit(solution)/shard_map/all_to_all | solution.py:172
  57.5 4.8 %all-to-all-start.1 = ((f32[64,1,256]{2,1,0:T(1,128)}), f32[64,1,256]{2,1,0:T(1,128)S(1)}, u32[]{:S(2)}, u32[]{:S(2)}) async-start(f32[64,1,256]{2,1,0:T(1,128)} %reshape.21114), calls=%async_computation.1 | async-start | bytes 131072 | tf_op jit(solution)/shard_map/all_to_all | solution.py:168
  62.3 0.8 reduce.14
  63.1 0.1 reshape.21113
  63.3 0.1 all_to_all.45
  63.4 9.5 %all-to-all-done.1 = f32[64,1,256]{2,1,0:T(1,128)S(1)} async-done(((f32[64,1,256]{2,1,0:T(1,128)}), f32[64,1,256]{2,1,0:T(1,128)S(1)}, u32[]{:S(2)}, u32[]{:S(2)}) %all-to-all-start.1) | async-done | bytes 65568 | tf_op jit(solution)/shard_map/all_to_all | solution.py:168
  72.9 0.8 reduce.16
  73.7 0.1 reshape.21115
  73.9 0.1 all_to_all.49
  74.6 0.1 fusion.2
  75.4 0.2 fusion.6
  76.4 0.2 fusion.10
  77.4 0.2 fusion.14
  78.4 0.2 fusion.18
  79.4 0.2 fusion.22
  80.4 0.2 fusion.26
  81.1 0.1 fusion.30
  81.5 0.1 fusion.34
  81.8 0.1 fusion.38
  82.2 0.1 fusion.42
  85.3 0.1 reshape.21116
  85.5 14.6 %all_to_all.59 = f32[64,1,256]{2,1,0:T(1,128)S(1)} all-to-all(f32[64,1,256]{2,1,0:T(1,128)S(1)} %reshape.21116), channel_id=1, replica_groups=mesh['xg'=4,'yd'=64] {'yd'}, dimensions={0} | all-to-all | bytes 131072 | tf_op jit(solution)/shard_map/all_to_all | solution.py:175
  100.1 0.8 reduce.17
  100.9 0.1 reshape.21117
  101.0 0.7 copy.234
  (256 shorter events, 12.9 us)
Async XLA Ops:
  0.9 15.2 %copy-start.1 = (f32[4,64,1,256]{3,2,1,0:T(1,128)S(1)}, f32[4,64,1,256]{3,2,1,0:T(1,128)}, u32[]{:S(2)}) copy-start(f32[4,64,1,256]{3,2,1,0:T(1,128)} %param.11) | copy-start | bytes 786436
  1.7 12.9 %copy-start.3 = (f32[64,1,256]{2,1,0:T(1,128)S(1)}, f32[64,1,256]{2,1,0:T(1,128)}, u32[]{:S(2)}) copy-start(f32[64,1,256]{2,1,0:T(1,128)} %param.10) | copy-start | bytes 196612
  1.7 33.7 %all-to-all-start.2 = ((f32[64,1,256]{2,1,0:T(1,128)}), f32[64,1,256]{2,1,0:T(1,128)S(1)}, u32[]{:S(2)}, u32[]{:S(2)}) async-start(f32[64,1,256]{2,1,0:T(1,128)} %reshape.21110), calls=%async_computation.2 | async-start | bytes 131072 | tf_op jit(solution)/shard_map/all_to_all | solution.py:169
  14.7 0.8 copy-start
  15.5 0.7 copy-start.4
  15.5 0.7 copy-start.5
  17.0 0.8 copy-start.2
  23.5 3.1 %collective-permute-start.1 = (f32[3,64,1]{1,2,0:T(1,128)S(1)}, f32[3,64,1]{1,2,0:T(1,128)S(1)}, u32[]{:S(2)}, u32[]{:S(2)}) collective-permute-start(f32[3,64,1]{1,2,0:T(1,128)S(1)} %squeeze.95), channel_id=1, source_target_pairs={{0,192},{64,0},{128,64},{192,128},{1,193},{65,1},{129,65},{193,129... | collective-permute-start | bytes 2312 | tf_op jit(solution)/shard_map/ppermute | solution.py:11
  24.1 2.4 %collective-permute-start = (f32[64,1]{0,1:T(1,128)S(1)}, f32[64,1]{0,1:T(1,128)S(1)}, u32[]{:S(2)}, u32[]{:S(2)}) collective-permute-start(f32[64,1]{0,1:T(1,128)S(1)} %bitcast.660), channel_id=1, source_target_pairs={{0,192},{64,0},{128,64},{192,128},{1,193},{65,1},{129,65},{193,129... | collective-permute-start | bytes 776 | tf_op jit(solution)/shard_map/ppermute | solution.py:11
  35.5 22.1 %all-to-all-start = ((f32[64,1,256]{2,1,0:T(1,128)}), f32[64,1,256]{2,1,0:T(1,128)S(1)}, u32[]{:S(2)}, u32[]{:S(2)}) async-start(f32[64,1,256]{2,1,0:T(1,128)} %reshape.21112), calls=%async_computation | async-start | bytes 131072 | tf_op jit(solution)/shard_map/all_to_all | solution.py:172
  57.5 15.4 %all-to-all-start.1 = ((f32[64,1,256]{2,1,0:T(1,128)}), f32[64,1,256]{2,1,0:T(1,128)S(1)}, u32[]{:S(2)}, u32[]{:S(2)}) async-start(f32[64,1,256]{2,1,0:T(1,128)} %reshape.21114), calls=%async_computation.1 | async-start | bytes 131072 | tf_op jit(solution)/shard_map/all_to_all | solution.py:168
